TPU v7x, 512 devices: a whole 4x4x16 slice. The times are simulated.
512 devices in a mesh: gz: 16 (over z), gy: 32 (over x, y, core).
Axes of the slice: x: 4, y: 4, z: 16, core: 2. Of those that a mesh axis runs over, the one named last changes fastest.
Arguments:
- tracer: float32 [512, 1024, 128], P('gz', 'gy'), may hold values from 0.1 to 10
- y_speed: float32 [512, 1024, 128], P('gz', 'gy'), may hold values from -0.4 to 0.4
- z_speed: float32 [512, 1024, 128], P('gz', 'gy'), may hold values from -0.4 to 0.4
- kappa: float32 [512, 1024, 128], P('gz', 'gy'), may hold values from 0.5 to 8
Outputs:
- updated: float32 [512, 1024, 128], P('gz', 'gy')
All inputs are finite; a program needn't handle non-finite values.
Results may differ from a plain program's by a relative error of at most 0.0003.
Values sent between devices are 32-bit elements; how exact they have to be, the bound alone decides.
A program may use at most 64 MiB of HBM per device.

v0:
```python
import jax
import jax.numpy as jnp
from jax import lax
from jax.sharding import PartitionSpec as P

NSUB = 4
rate_const = 500.0


def padded_2(x, sides, width):
    for axis, dim in sides:
        peers, length = (lax.axis_size(axis), x.shape[dim])
        up = [(i, (i + 1) % peers) for i in range(peers - 1)]
        down = [(j, i) for i, j in up]
        last = lax.slice_in_dim(x, length - width, length, axis=dim)
        leading = lax.slice_in_dim(x, 0, width, axis=dim)
        before = lax.ppermute(last, axis, up)
        after = lax.ppermute(leading, axis, down)
        x = jnp.concatenate([before, x, after], axis=dim)
    return x


def from_behind(x, axis, by):
    peers = lax.axis_size(axis)
    pairs = [(i, i + by) for i in range(peers) if 0 <= i + by < peers]
    return lax.ppermute(x, axis, pairs)


def advect_once(tracer, y_speed, z_speed):
    face_y = 0.5 * (y_speed[:, 1:] + y_speed[:, :-1])
    flux_y = jnp.maximum(face_y, 0.0) * tracer[:, :-1] + jnp.minimum(face_y, 0.0) * tracer[:, 1:]
    diff_y = flux_y[:, 1:] - flux_y[:, :-1]
    face_z = 0.5 * (z_speed[1:] + z_speed[:-1])
    flux_z = jnp.maximum(face_z, 0.0) * tracer[:-1] + jnp.minimum(face_z, 0.0) * tracer[1:]
    diff_z = flux_z[1:] - flux_z[:-1]
    return tracer[1:-1, 1:-1] - diff_y[1:-1] - diff_z[:, 1:-1]


def move_down(values, offset, axis, fill):
    count = values.shape[axis]
    kept = lax.slice_in_dim(values, 0, count - offset, axis=axis)
    padding = jnp.full_like(lax.slice_in_dim(values, 0, offset, axis=axis), fill)
    return jnp.concatenate([padding, kept], axis=axis)


def move_up(values, offset, axis, fill):
    count = values.shape[axis]
    kept = lax.slice_in_dim(values, offset, count, axis=axis)
    padding = jnp.full_like(lax.slice_in_dim(values, 0, offset, axis=axis), fill)
    return jnp.concatenate([kept, padding], axis=axis)


def reduce_lines(sub_diag, main_diag, sup_diag, rights, axis):
    count = main_diag.shape[axis]
    offset = 1
    while offset < count:
        factor_low = -sub_diag / move_down(main_diag, offset, axis, 1.0)
        factor_high = -sup_diag / move_up(main_diag, offset, axis, 1.0)
        new_main = (
            main_diag
            + factor_low * move_down(sup_diag, offset, axis, 0.0)
            + factor_high * move_up(sub_diag, offset, axis, 0.0)
        )
        new_sub = factor_low * move_down(sub_diag, offset, axis, 0.0)
        new_sup = factor_high * move_up(sup_diag, offset, axis, 0.0)
        rights = tuple(
            (
                right
                + factor_low * move_down(right, offset, axis, 0.0)
                + factor_high * move_up(right, offset, axis, 0.0)
                for right in rights
            )
        )
        sub_diag, main_diag, sup_diag = (new_sub, new_main, new_sup)
        offset = offset * 2
    return tuple((right / main_diag for right in rights))


def solve_rows(items):
    tracer_part, kappa_part = items
    count = kappa_part.shape[1]
    inner = rate_const * 0.5 * (kappa_part[:, 1:] + kappa_part[:, :-1])
    lower = jnp.concatenate([rate_const * kappa_part[:, :1], inner], axis=1)
    upper = jnp.concatenate([inner, rate_const * kappa_part[:, count - 1 :]], axis=1)
    main_diag = 1.0 + lower + upper
    zero_row = jnp.zeros_like(kappa_part[:, :1])
    sub_diag = jnp.concatenate([zero_row, -inner], axis=1)
    sup_diag = jnp.concatenate([-inner, zero_row], axis=1)
    solved = reduce_lines(sub_diag, main_diag, sup_diag, (tracer_part,), 1)[0]
    return lax.all_to_all(solved, "gy", split_axis=1, concat_axis=0, tiled=True)


def local(tracer, y_speed, z_speed, kappa):
    depth_z, depth_y, band = tracer.shape
    z_index = lax.axis_index("gz")
    z_count = lax.axis_size("gz")
    fields = jnp.stack([y_speed, z_speed, kappa])
    width = 1
    padded = padded_2(fields, (("gz", 1), ("gy", 2)), 1)
    state = tracer
    for step in range(NSUB):
        rimmed = padded_2(state, (("gz", 0), ("gy", 1)), 1)
        state = advect_once(rimmed, padded[0], padded[1])
    kappa_below = padded[2, width - 1 : width, width : width + depth_y]
    kappa_above = padded[2, width + depth_z : width + depth_z + 1, width : width + depth_y]
    lines = solve_rows(
        (
            lax.all_to_all(state, "gy", split_axis=0, concat_axis=1, tiled=True),
            lax.all_to_all(kappa, "gy", split_axis=0, concat_axis=1, tiled=True),
        )
    )
    inner = rate_const * 0.5 * (kappa[1:] + kappa[:-1])
    low_edge = jnp.where(
        z_index == 0, rate_const * kappa[:1], rate_const * 0.5 * (kappa[:1] + kappa_below)
    )
    high_edge = jnp.where(
        z_index == z_count - 1,
        rate_const * kappa[depth_z - 1 :],
        rate_const * 0.5 * (kappa[depth_z - 1 :] + kappa_above),
    )
    lower = jnp.concatenate([low_edge, inner], axis=0)
    upper = jnp.concatenate([inner, high_edge], axis=0)
    main_diag = 1.0 + lower + upper
    inner_count = depth_z - 1
    zero_row = jnp.zeros_like(kappa[:1])
    sub_local = jnp.concatenate([zero_row, -lower[1:inner_count]], axis=0)
    sup_local = jnp.concatenate([-upper[: inner_count - 1], zero_row], axis=0)
    zero_rows = jnp.zeros_like(kappa[: inner_count - 1])
    first_right = jnp.concatenate([lower[:1], zero_rows], axis=0)
    last_right = jnp.concatenate([zero_rows, upper[inner_count - 1 : inner_count]], axis=0)
    base, toward_low, toward_high = reduce_lines(
        sub_local,
        main_diag[:inner_count],
        sup_local,
        (lines[:inner_count], first_right, last_right),
        0,
    )
    following = from_behind(jnp.stack([base[0], toward_low[0], toward_high[0]]), "gz", -1)
    sep_low = lower[depth_z - 1]
    sep_high = upper[depth_z - 1]
    sub_red = jnp.where(z_index == 0, 0.0, -sep_low * toward_low[inner_count - 1])
    diag_red = (
        main_diag[depth_z - 1] - sep_low * toward_high[inner_count - 1] - sep_high * following[1]
    )
    sup_red = -sep_high * following[2]
    rhs_red = lines[depth_z - 1] + sep_low * base[inner_count - 1] + sep_high * following[0]
    equations = jnp.stack([sub_red, diag_red, sup_red, rhs_red])
    collected = lax.all_gather(equations[None], "gz", axis=0, tiled=True)
    values = reduce_lines(collected[:, 0], collected[:, 1], collected[:, 2], (collected[:, 3],), 0)[
        0
    ]
    sep_here = lax.dynamic_index_in_dim(values, z_index, axis=0, keepdims=False)
    previous = lax.dynamic_index_in_dim(values, jnp.maximum(z_index - 1, 0), axis=0, keepdims=False)
    sep_prev = jnp.where(z_index > 0, previous, 0.0)
    interior = base + sep_prev[None] * toward_low + sep_here[None] * toward_high
    return jnp.concatenate([interior, sep_here[None]], axis=0)


def solution(mesh):
    return jax.shard_map(
        local,
        mesh=mesh,
        in_specs=(
            P("gz", "gy", None),
            P("gz", "gy", None),
            P("gz", "gy", None),
            P("gz", "gy", None),
        ),
        out_specs=P("gz", "gy", None),
        check_vma=False,
    )
```

profile of v0, /device:TPU:2, one launch (start us, length us, event | category | flops | bytes accessed | tf_op | source)
XLA Modules:
  0.0 254.8 jit_solution(3350201011597019658)
XLA Ops:
  6.5 0.9 fusion.100
  7.4 3.8 %collective-permute-start.4 = (f32[1,32,128]{2,1,0:T(8,128)S(1)}, f32[1,32,128]{2,1,0:T(8,128)S(1)}, u32[]{:S(2)}, u32[]{:S(2)}) collective-permute-start(f32[1,32,128]{2,1,0:T(8,128)S(1)} %get-tuple-element.204), channel_id=1, source_target_pairs={{0,32},{32,64},{64,96},{96,128},{128,160},{160,192},{192,224},{224... | collective-permute-start | bytes 49160 | tf_op jit(solution)/shard_map/ppermute | solution.py:17
  11.2 0.8 pad_maximum_fusion.14
  12.0 3.8 %collective-permute-start = (f32[3,1,32,128]{3,2,1,0:T(8,128)S(1)}, f32[3,1,32,128]{3,2,1,0:T(8,128)S(1)}, u32[]{:S(2)}, u32[]{:S(2)}) collective-permute-start(f32[3,1,32,128]{3,2,1,0:T(8,128)S(1)} %get-tuple-element.65), channel_id=1, source_target_pairs={{0,32},{32,64},{64,96},{96,128},{128,160},{160,192},{192,224},{224... | collective-permute-start | bytes 147464 | tf_op jit(solution)/shard_map/ppermute | solution.py:17
  15.9 1.3 collective-permute-start.1
  17.2 1.3 collective-permute-start.5
  18.5 4.9 %collective-permute-done.5 = f32[1,32,128]{2,1,0:T(8,128)S(1)} collective-permute-done((f32[1,32,128]{2,1,0:T(8,128)S(1)}, f32[1,32,128]{2,1,0:T(8,128)S(1)}, u32[]{:S(2)}, u32[]{:S(2)}) %collective-permute-start.5) | collective-permute-done | bytes 16416 | tf_op jit(solution)/shard_map/ppermute | solution.py:18
  23.5 1.9 collective-permute-start.6
  25.4 5.8 %collective-permute-start.7 = (f32[34,1,128]{2,1,0:T(1,128)S(1)}, f32[34,1,128]{2,1,0:T(1,128)S(1)}, u32[]{:S(2)}, u32[]{:S(2)}) collective-permute-start(f32[34,1,128]{2,1,0:T(1,128)S(1)} %get-tuple-element.114), channel_id=1, source_target_pairs={{1,0},{2,1},{3,2},{4,3},{5,4},{6,5},{7,6},{8,7},{9,8},{10,9},{11,1... | collective-permute-start | bytes 52232 | tf_op jit(solution)/shard_map/ppermute | solution.py:18
  31.2 1.1 pad_maximum_fusion.11
  32.2 1.9 collective-permute-start.2
  34.2 5.8 %collective-permute-start.3 = (f32[3,34,1,128]{3,2,1,0:T(1,128)S(1)}, f32[3,34,1,128]{3,2,1,0:T(1,128)S(1)}, u32[]{:S(2)}, u32[]{:S(2)}) collective-permute-start(f32[3,34,1,128]{3,2,1,0:T(1,128)S(1)} %get-tuple-element.62), channel_id=1, source_target_pairs={{1,0},{2,1},{3,2},{4,3},{5,4},{6,5},{7,6},{8,7},{9,8},{10,9},{11,1... | collective-permute-start | bytes 156680 | tf_op jit(solution)/shard_map/ppermute | solution.py:18
  40.1 1.6 collective-permute-done.3
  41.7 1.4 pad_maximum_fusion
  44.1 4.9 %collective-permute-start.8 = (f32[1,32,128]{2,1,0:T(8,128)S(1)}, f32[1,32,128]{2,1,0:T(8,128)S(1)}, u32[]{:S(2)}, u32[]{:S(2)}) collective-permute-start(f32[1,32,128]{2,1,0:T(8,128)S(1)} %get-tuple-element.201), channel_id=1, source_target_pairs={{0,32},{32,64},{64,96},{96,128},{128,160},{160,192},{192,224},{224... | collective-permute-start | bytes 49160 | tf_op jit(solution)/shard_map/ppermute | solution.py:17
  49.1 1.3 collective-permute-start.9
  50.4 7.8 %all-to-all-start.1 = ((f32[32,32,128]{2,1,0:T(8,128)}), f32[32,32,128]{2,1,0:T(8,128)S(1)}, u32[]{:S(2)}, u32[]{:S(2)}) async-start(f32[32,32,128]{2,1,0:T(8,128)} %param.7), calls=%async_computation.1 | async-start | bytes 1048576 | tf_op jit(solution)/shard_map/all_to_all | solution.py:109
  58.2 2.0 collective-permute-start.10
  60.3 5.6 %collective-permute-start.11 = (f32[34,1,128]{2,1,0:T(1,128)S(1)}, f32[34,1,128]{2,1,0:T(1,128)S(1)}, u32[]{:S(2)}, u32[]{:S(2)}) collective-permute-start(f32[34,1,128]{2,1,0:T(1,128)S(1)} %get-tuple-element.112), channel_id=1, source_target_pairs={{1,0},{2,1},{3,2},{4,3},{5,4},{6,5},{7,6},{8,7},{9,8},{10,9},{11,1... | collective-permute-start | bytes 52232 | tf_op jit(solution)/shard_map/ppermute | solution.py:18
  65.9 1.3 add_multiply_fusion
  67.2 0.4 collective-permute-done.10
  68.6 4.6 %collective-permute-start.12 = (f32[1,32,128]{2,1,0:T(8,128)S(1)}, f32[1,32,128]{2,1,0:T(8,128)S(1)}, u32[]{:S(2)}, u32[]{:S(2)}) collective-permute-start(f32[1,32,128]{2,1,0:T(8,128)S(1)} %get-tuple-element.199), channel_id=1, source_target_pairs={{0,32},{32,64},{64,96},{96,128},{128,160},{160,192},{192,224},{224... | collective-permute-start | bytes 49160 | tf_op jit(solution)/shard_map/ppermute | solution.py:17
  73.1 1.3 collective-permute-start.13
  74.5 5.4 %collective-permute-done.13 = f32[1,32,128]{2,1,0:T(8,128)S(1)} collective-permute-done((f32[1,32,128]{2,1,0:T(8,128)S(1)}, f32[1,32,128]{2,1,0:T(8,128)S(1)}, u32[]{:S(2)}, u32[]{:S(2)}) %collective-permute-start.13) | collective-permute-done | bytes 16416 | tf_op jit(solution)/shard_map/ppermute | solution.py:18
  80.0 1.9 collective-permute-start.14
  81.9 5.8 %collective-permute-start.15 = (f32[34,1,128]{2,1,0:T(1,128)S(1)}, f32[34,1,128]{2,1,0:T(1,128)S(1)}, u32[]{:S(2)}, u32[]{:S(2)}) collective-permute-start(f32[34,1,128]{2,1,0:T(1,128)S(1)} %get-tuple-element.110), channel_id=1, source_target_pairs={{1,0},{2,1},{3,2},{4,3},{5,4},{6,5},{7,6},{8,7},{9,8},{10,9},{11,1... | collective-permute-start | bytes 52232 | tf_op jit(solution)/shard_map/ppermute | solution.py:18
  87.7 1.1 pad_slice_fusion.2
  90.0 3.9 %collective-permute-start.16 = (f32[1,32,128]{2,1,0:T(8,128)S(1)}, f32[1,32,128]{2,1,0:T(8,128)S(1)}, u32[]{:S(2)}, u32[]{:S(2)}) collective-permute-start(f32[1,32,128]{2,1,0:T(8,128)S(1)} %get-tuple-element.197), channel_id=1, source_target_pairs={{0,32},{32,64},{64,96},{96,128},{128,160},{160,192},{192,224},{224... | collective-permute-start | bytes 49160 | tf_op jit(solution)/shard_map/ppermute | solution.py:17
  93.9 1.3 collective-permute-start.17
  95.2 0.8 pad_slice_fusion
  96.1 4.3 %collective-permute-done.17 = f32[1,32,128]{2,1,0:T(8,128)S(1)} collective-permute-done((f32[1,32,128]{2,1,0:T(8,128)S(1)}, f32[1,32,128]{2,1,0:T(8,128)S(1)}, u32[]{:S(2)}, u32[]{:S(2)}) %collective-permute-start.17) | collective-permute-done | bytes 16416 | tf_op jit(solution)/shard_map/ppermute | solution.py:18
  100.4 1.9 collective-permute-start.18
  102.4 5.8 %collective-permute-start.19 = (f32[34,1,128]{2,1,0:T(1,128)S(1)}, f32[34,1,128]{2,1,0:T(1,128)S(1)}, u32[]{:S(2)}, u32[]{:S(2)}) collective-permute-start(f32[34,1,128]{2,1,0:T(1,128)S(1)} %get-tuple-element.108), channel_id=1, source_target_pairs={{1,0},{2,1},{3,2},{4,3},{5,4},{6,5},{7,6},{8,7},{9,8},{10,9},{11,1... | collective-permute-start | bytes 52232 | tf_op jit(solution)/shard_map/ppermute | solution.py:18
  108.1 0.7 fusion.46
  108.9 0.7 collective-permute-done.19
  110.2 1.1 fusion.11
  111.3 8.0 %all-to-all-start = ((f32[32,32,128]{2,1,0:T(8,128)}), f32[32,32,128]{2,1,0:T(8,128)S(1)}, u32[]{:S(2)}, u32[]{:S(2)}) async-start(f32[32,32,128]{2,1,0:T(8,128)} %fusion.11), calls=%async_computation | async-start | bytes 1048576 | tf_op jit(solution)/shard_map/all_to_all | solution.py:108
  119.5 1.1 pad_slice_fusion.5
  120.7 8.5 %all-to-all-done = f32[32,32,128]{2,1,0:T(8,128)S(1)} async-done(((f32[32,32,128]{2,1,0:T(8,128)}), f32[32,32,128]{2,1,0:T(8,128)S(1)}, u32[]{:S(2)}, u32[]{:S(2)}) %all-to-all-start) | async-done | bytes 524320 | tf_op jit(solution)/shard_map/all_to_all | solution.py:108
  129.2 0.4 multiply_add_fusion.16
  129.8 0.9 copy-done.8
  130.8 0.5 multiply_add_fusion.15
  131.9 0.5 multiply_add_fusion.13
  132.9 0.4 multiply_add_fusion.11
  133.9 0.5 multiply_add_fusion.9
  135.0 0.5 multiply_add_fusion.7
  138.4 1.0 add_divide_fusion
  139.4 5.4 %all-to-all-start.2 = ((f32[1,1024,128]{2,0,1:T(1,128)}), f32[1,1024,128]{2,0,1:T(1,128)S(1)}, u32[]{:S(2)}, u32[]{:S(2)}) async-start(f32[1,1024,128]{2,0,1:T(1,128)} %bitcast.8), calls=%async_computation.2 | async-start | bytes 1048576 | tf_op jit(solution)/shard_map/all_to_all | solution.py:90
  145.2 0.9 fusion.60
  146.1 8.5 %all-to-all-done.2 = f32[1,1024,128]{2,0,1:T(1,128)S(1)} async-done(((f32[1,1024,128]{2,0,1:T(1,128)}), f32[1,1024,128]{2,0,1:T(1,128)S(1)}, u32[]{:S(2)}, u32[]{:S(2)}) %all-to-all-start.2) | async-done | bytes 524320 | tf_op jit(solution)/shard_map/all_to_all | solution.py:90
  154.7 0.9 copy-done.13
  156.5 0.8 copy-done.10
  157.6 0.7 multiply_add_fusion.31
  159.2 0.9 multiply_add_fusion.29
  161.0 0.8 multiply_add_fusion.27
  162.2 0.7 multiply_add_fusion.22
  163.0 0.5 add_divide_fusion.3
  164.1 1.3 collective-permute-start.20
  165.4 6.4 %collective-permute-done.20 = f32[3,32,128]{2,1,0:T(8,128)S(1)} collective-permute-done((f32[3,32,128]{2,1,0:T(8,128)S(1)}, f32[3,32,128]{2,1,0:T(8,128)S(1)}, u32[]{:S(2)}, u32[]{:S(2)}) %collective-permute-start.20) | collective-permute-done | bytes 49184 | tf_op jit(solution)/shard_map/ppermute | solution.py:26
  171.8 0.6 pad_maximum_fusion.6
  172.5 69.8 %all-gather.3.cloned.1.call-done = f32[64,32,128]{2,1,0:T(8,128)} async-done(((f32[4,32,128]{2,1,0:T(8,128)}), f32[64,32,128]{2,1,0:T(8,128)}) %all-gather.3.cloned.1.call-update) | async-done | bytes 1048592 | tf_op jit(solution)/shard_map/all_gather | solution.py:148
  242.3 1.9 slice_bitcast_fusion.11
  246.3 0.7 copy-done.7
  247.2 0.8 pad_maximum_fusion.5
  (187 shorter events, 15.9 us)
Async XLA Ops:
  6.5 11.9 %copy-start.5 = (f32[32,32,128]{2,1,0:T(8,128)S(1)}, f32[32,32,128]{2,1,0:T(8,128)}, u32[]{:S(2)}) copy-start(f32[32,32,128]{2,1,0:T(8,128)} %param.4) | copy-start | bytes 1572868
  6.5 24.6 %copy-start.2 = (f32[32,32,128]{2,1,0:T(8,128)S(1)}, f32[32,32,128]{2,1,0:T(8,128)}, u32[]{:S(2)}) copy-start(f32[32,32,128]{2,1,0:T(8,128)} %param.5) | copy-start | bytes 1572868
  6.5 24.6 %copy-start.1 = (f32[32,32,128]{2,1,0:T(8,128)S(1)}, f32[32,32,128]{2,1,0:T(8,128)}, u32[]{:S(2)}) copy-start(f32[32,32,128]{2,1,0:T(8,128)} %param.6) | copy-start | bytes 1572868
  7.4 11.1 %collective-permute-start.4 = (f32[1,32,128]{2,1,0:T(8,128)S(1)}, f32[1,32,128]{2,1,0:T(8,128)S(1)}, u32[]{:S(2)}, u32[]{:S(2)}) collective-permute-start(f32[1,32,128]{2,1,0:T(8,128)S(1)} %get-tuple-element.204), channel_id=1, source_target_pairs={{0,32},{32,64},{64,96},{96,128},{128,160},{160,192},{192,224},{224... | collective-permute-start | bytes 49160 | tf_op jit(solution)/shard_map/ppermute | solution.py:17
  12.0 19.1 %collective-permute-start = (f32[3,1,32,128]{3,2,1,0:T(8,128)S(1)}, f32[3,1,32,128]{3,2,1,0:T(8,128)S(1)}, u32[]{:S(2)}, u32[]{:S(2)}) collective-permute-start(f32[3,1,32,128]{3,2,1,0:T(8,128)S(1)} %get-tuple-element.65), channel_id=1, source_target_pairs={{0,32},{32,64},{64,96},{96,128},{128,160},{160,192},{192,224},{224... | collective-permute-start | bytes 147464 | tf_op jit(solution)/shard_map/ppermute | solution.py:17
  15.9 15.3 %collective-permute-start.1 = (f32[3,1,32,128]{3,2,1,0:T(8,128)S(1)}, f32[3,1,32,128]{3,2,1,0:T(8,128)S(1)}, u32[]{:S(2)}, u32[]{:S(2)}) collective-permute-start(f32[3,1,32,128]{3,2,1,0:T(8,128)S(1)} %get-tuple-element.66), channel_id=1, source_target_pairs={{32,0},{64,32},{96,64},{128,96},{160,128},{192,160},{224,192},{256... | collective-permute-start | bytes 147464 | tf_op jit(solution)/shard_map/ppermute | solution.py:18
  17.2 6.3 %collective-permute-start.5 = (f32[1,32,128]{2,1,0:T(8,128)S(1)}, f32[1,32,128]{2,1,0:T(8,128)S(1)}, u32[]{:S(2)}, u32[]{:S(2)}) collective-permute-start(f32[1,32,128]{2,1,0:T(8,128)S(1)} %get-tuple-element.203), channel_id=1, source_target_pairs={{32,0},{64,32},{96,64},{128,96},{160,128},{192,160},{224,192},{256... | collective-permute-start | bytes 49160 | tf_op jit(solution)/shard_map/ppermute | solution.py:18
  23.5 16.5 %collective-permute-start.6 = (f32[34,1,128]{2,1,0:T(1,128)S(1)}, f32[34,1,128]{2,1,0:T(1,128)S(1)}, u32[]{:S(2)}, u32[]{:S(2)}) collective-permute-start(f32[34,1,128]{2,1,0:T(1,128)S(1)} %get-tuple-element.113), channel_id=1, source_target_pairs={{0,1},{1,2},{2,3},{3,4},{4,5},{5,6},{6,7},{7,8},{8,9},{9,10},{10,1... | collective-permute-start | bytes 52232 | tf_op jit(solution)/shard_map/ppermute | solution.py:17
  25.4 14.6 %collective-permute-start.7 = (f32[34,1,128]{2,1,0:T(1,128)S(1)}, f32[34,1,128]{2,1,0:T(1,128)S(1)}, u32[]{:S(2)}, u32[]{:S(2)}) collective-permute-start(f32[34,1,128]{2,1,0:T(1,128)S(1)} %get-tuple-element.114), channel_id=1, source_target_pairs={{1,0},{2,1},{3,2},{4,3},{5,4},{6,5},{7,6},{8,7},{9,8},{10,9},{11,1... | collective-permute-start | bytes 52232 | tf_op jit(solution)/shard_map/ppermute | solution.py:18
  32.2 7.8 %collective-permute-start.2 = (f32[3,34,1,128]{3,2,1,0:T(1,128)S(1)}, f32[3,34,1,128]{3,2,1,0:T(1,128)S(1)}, u32[]{:S(2)}, u32[]{:S(2)}) collective-permute-start(f32[3,34,1,128]{3,2,1,0:T(1,128)S(1)} %get-tuple-element.61), channel_id=1, source_target_pairs={{0,1},{1,2},{2,3},{3,4},{4,5},{5,6},{6,7},{7,8},{8,9},{9,10},{10,1... | collective-permute-start | bytes 156680 | tf_op jit(solution)/shard_map/ppermute | solution.py:17
  34.2 7.5 %collective-permute-start.3 = (f32[3,34,1,128]{3,2,1,0:T(1,128)S(1)}, f32[3,34,1,128]{3,2,1,0:T(1,128)S(1)}, u32[]{:S(2)}, u32[]{:S(2)}) collective-permute-start(f32[3,34,1,128]{3,2,1,0:T(1,128)S(1)} %get-tuple-element.62), channel_id=1, source_target_pairs={{1,0},{2,1},{3,2},{4,3},{5,4},{6,5},{7,6},{8,7},{9,8},{10,9},{11,1... | collective-permute-start | bytes 156680 | tf_op jit(solution)/shard_map/ppermute | solution.py:18
  44.1 14.0 %collective-permute-start.8 = (f32[1,32,128]{2,1,0:T(8,128)S(1)}, f32[1,32,128]{2,1,0:T(8,128)S(1)}, u32[]{:S(2)}, u32[]{:S(2)}) collective-permute-start(f32[1,32,128]{2,1,0:T(8,128)S(1)} %get-tuple-element.201), channel_id=1, source_target_pairs={{0,32},{32,64},{64,96},{96,128},{128,160},{160,192},{192,224},{224... | collective-permute-start | bytes 49160 | tf_op jit(solution)/shard_map/ppermute | solution.py:17
  49.1 9.1 %collective-permute-start.9 = (f32[1,32,128]{2,1,0:T(8,128)S(1)}, f32[1,32,128]{2,1,0:T(8,128)S(1)}, u32[]{:S(2)}, u32[]{:S(2)}) collective-permute-start(f32[1,32,128]{2,1,0:T(8,128)S(1)} %get-tuple-element.202), channel_id=1, source_target_pairs={{32,0},{64,32},{96,64},{128,96},{160,128},{192,160},{224,192},{256... | collective-permute-start | bytes 49160 | tf_op jit(solution)/shard_map/ppermute | solution.py:18
  50.4 60.9 %all-to-all-start.1 = ((f32[32,32,128]{2,1,0:T(8,128)}), f32[32,32,128]{2,1,0:T(8,128)S(1)}, u32[]{:S(2)}, u32[]{:S(2)}) async-start(f32[32,32,128]{2,1,0:T(8,128)} %param.7), calls=%async_computation.1 | async-start | bytes 1048576 | tf_op jit(solution)/shard_map/all_to_all | solution.py:109
  58.2 9.4 %collective-permute-start.10 = (f32[34,1,128]{2,1,0:T(1,128)S(1)}, f32[34,1,128]{2,1,0:T(1,128)S(1)}, u32[]{:S(2)}, u32[]{:S(2)}) collective-permute-start(f32[34,1,128]{2,1,0:T(1,128)S(1)} %get-tuple-element.111), channel_id=1, source_target_pairs={{0,1},{1,2},{2,3},{3,4},{4,5},{5,6},{6,7},{7,8},{8,9},{9,10},{10,1... | collective-permute-start | bytes 52232 | tf_op jit(solution)/shard_map/ppermute | solution.py:17
  60.3 7.4 %collective-permute-start.11 = (f32[34,1,128]{2,1,0:T(1,128)S(1)}, f32[34,1,128]{2,1,0:T(1,128)S(1)}, u32[]{:S(2)}, u32[]{:S(2)}) collective-permute-start(f32[34,1,128]{2,1,0:T(1,128)S(1)} %get-tuple-element.112), channel_id=1, source_target_pairs={{1,0},{2,1},{3,2},{4,3},{5,4},{6,5},{7,6},{8,7},{9,8},{10,9},{11,1... | collective-permute-start | bytes 52232 | tf_op jit(solution)/shard_map/ppermute | solution.py:18
  67.2 21.6 %copy-start.3 = (f32[31,32,128]{2,1,0:T(8,128)}, f32[31,32,128]{2,1,0:T(8,128)S(1)}, u32[]{:S(2)}) copy-start(f32[31,32,128]{2,1,0:T(8,128)S(1)} %add_multiply_fusion) | copy-start | bytes 1523716
  68.6 6.0 %collective-permute-start.12 = (f32[1,32,128]{2,1,0:T(8,128)S(1)}, f32[1,32,128]{2,1,0:T(8,128)S(1)}, u32[]{:S(2)}, u32[]{:S(2)}) collective-permute-start(f32[1,32,128]{2,1,0:T(8,128)S(1)} %get-tuple-element.199), channel_id=1, source_target_pairs={{0,32},{32,64},{64,96},{96,128},{128,160},{160,192},{192,224},{224... | collective-permute-start | bytes 49160 | tf_op jit(solution)/shard_map/ppermute | solution.py:17
  73.1 6.8 %collective-permute-start.13 = (f32[1,32,128]{2,1,0:T(8,128)S(1)}, f32[1,32,128]{2,1,0:T(8,128)S(1)}, u32[]{:S(2)}, u32[]{:S(2)}) collective-permute-start(f32[1,32,128]{2,1,0:T(8,128)S(1)} %get-tuple-element.200), channel_id=1, source_target_pairs={{32,0},{64,32},{96,64},{128,96},{160,128},{192,160},{224,192},{256... | collective-permute-start | bytes 49160 | tf_op jit(solution)/shard_map/ppermute | solution.py:18
  80.0 8.8 %collective-permute-start.14 = (f32[34,1,128]{2,1,0:T(1,128)S(1)}, f32[34,1,128]{2,1,0:T(1,128)S(1)}, u32[]{:S(2)}, u32[]{:S(2)}) collective-permute-start(f32[34,1,128]{2,1,0:T(1,128)S(1)} %get-tuple-element.109), channel_id=1, source_target_pairs={{0,1},{1,2},{2,3},{3,4},{4,5},{5,6},{6,7},{7,8},{8,9},{9,10},{10,1... | collective-permute-start | bytes 52232 | tf_op jit(solution)/shard_map/ppermute | solution.py:17
  81.9 7.2 %collective-permute-start.15 = (f32[34,1,128]{2,1,0:T(1,128)S(1)}, f32[34,1,128]{2,1,0:T(1,128)S(1)}, u32[]{:S(2)}, u32[]{:S(2)}) collective-permute-start(f32[34,1,128]{2,1,0:T(1,128)S(1)} %get-tuple-element.110), channel_id=1, source_target_pairs={{1,0},{2,1},{3,2},{4,3},{5,4},{6,5},{7,6},{8,7},{9,8},{10,9},{11,1... | collective-permute-start | bytes 52232 | tf_op jit(solution)/shard_map/ppermute | solution.py:18
  90.0 6.1 %collective-permute-start.16 = (f32[1,32,128]{2,1,0:T(8,128)S(1)}, f32[1,32,128]{2,1,0:T(8,128)S(1)}, u32[]{:S(2)}, u32[]{:S(2)}) collective-permute-start(f32[1,32,128]{2,1,0:T(8,128)S(1)} %get-tuple-element.197), channel_id=1, source_target_pairs={{0,32},{32,64},{64,96},{96,128},{128,160},{160,192},{192,224},{224... | collective-permute-start | bytes 49160 | tf_op jit(solution)/shard_map/ppermute | solution.py:17
  93.9 6.5 %collective-permute-start.17 = (f32[1,32,128]{2,1,0:T(8,128)S(1)}, f32[1,32,128]{2,1,0:T(8,128)S(1)}, u32[]{:S(2)}, u32[]{:S(2)}) collective-permute-start(f32[1,32,128]{2,1,0:T(8,128)S(1)} %get-tuple-element.198), channel_id=1, source_target_pairs={{32,0},{64,32},{96,64},{128,96},{160,128},{192,160},{224,192},{256... | collective-permute-start | bytes 49160 | tf_op jit(solution)/shard_map/ppermute | solution.py:18
  100.4 8.4 %collective-permute-start.18 = (f32[34,1,128]{2,1,0:T(1,128)S(1)}, f32[34,1,128]{2,1,0:T(1,128)S(1)}, u32[]{:S(2)}, u32[]{:S(2)}) collective-permute-start(f32[34,1,128]{2,1,0:T(1,128)S(1)} %get-tuple-element.107), channel_id=1, source_target_pairs={{0,1},{1,2},{2,3},{3,4},{4,5},{5,6},{6,7},{7,8},{8,9},{9,10},{10,1... | collective-permute-start | bytes 52232 | tf_op jit(solution)/shard_map/ppermute | solution.py:17
  102.4 7.2 %collective-permute-start.19 = (f32[34,1,128]{2,1,0:T(1,128)S(1)}, f32[34,1,128]{2,1,0:T(1,128)S(1)}, u32[]{:S(2)}, u32[]{:S(2)}) collective-permute-start(f32[34,1,128]{2,1,0:T(1,128)S(1)} %get-tuple-element.108), channel_id=1, source_target_pairs={{1,0},{2,1},{3,2},{4,3},{5,4},{6,5},{7,6},{8,7},{9,8},{10,9},{11,1... | collective-permute-start | bytes 52232 | tf_op jit(solution)/shard_map/ppermute | solution.py:18
  111.3 17.8 %all-to-all-start = ((f32[32,32,128]{2,1,0:T(8,128)}), f32[32,32,128]{2,1,0:T(8,128)S(1)}, u32[]{:S(2)}, u32[]{:S(2)}) async-start(f32[32,32,128]{2,1,0:T(8,128)} %fusion.11), calls=%async_computation | async-start | bytes 1048576 | tf_op jit(solution)/shard_map/all_to_all | solution.py:108
  129.6 1.0 copy-start.8
  129.6 1.2 copy-start.9
  138.3 6.8 %copy-start.4 = (f32[31,32,128]{2,1,0:T(8,128)S(1)}, f32[31,32,128]{2,1,0:T(8,128)}, u32[]{:S(2)}) copy-start(f32[31,32,128]{2,1,0:T(8,128)} %copy-done.3) | copy-start | bytes 1523716
  139.4 15.2 %all-to-all-start.2 = ((f32[1,1024,128]{2,0,1:T(1,128)}), f32[1,1024,128]{2,0,1:T(1,128)S(1)}, u32[]{:S(2)}, u32[]{:S(2)}) async-start(f32[1,1024,128]{2,0,1:T(1,128)} %bitcast.8), calls=%async_computation.2 | async-start | bytes 1048576 | tf_op jit(solution)/shard_map/all_to_all | solution.py:90
  144.8 97.5 %all-gather.3.cloned.1.call-start = ((), (), s32[]{:S(2)}) async-start(), calls=%async_computation.3 | async-start | bytes 1114112 | tf_op jit(solution)/shard_map/all_gather | solution.py:148
  154.6 1.0 copy-start.13
  156.2 1.0 copy-start.10
  156.2 1.2 copy-start.11
  156.3 1.3 copy-start.12
  163.6 8.2 %copy-start.6 = (f32[31,32,128]{2,1,0:T(8,128)}, f32[31,32,128]{2,1,0:T(8,128)S(1)}, u32[]{:S(2)}) copy-start(f32[31,32,128]{2,1,0:T(8,128)S(1)} %get-tuple-element.60) | copy-start | bytes 1523716
  164.1 7.7 %collective-permute-start.20 = (f32[3,32,128]{2,1,0:T(8,128)S(1)}, f32[3,32,128]{2,1,0:T(8,128)S(1)}, u32[]{:S(2)}, u32[]{:S(2)}) collective-permute-start(f32[3,32,128]{2,1,0:T(8,128)S(1)} %pad_maximum_fusion.15), channel_id=1, source_target_pairs={{32,0},{64,32},{96,64},{128,96},{160,128},{192,160},{224,192},{256... | collective-permute-start | bytes 147464 | tf_op jit(solution)/shard_map/ppermute | solution.py:26
  242.3 2.0 copy-start
  245.9 1.0 copy-start.7
Sparse Core Ops, SparseCore 0:
  172.6 69.6 all-gather.2
where the time goes:
time: 256 us; the launch traced here: 255 us
  waiting for transfers between devices  111 us (43%)
  starting transfers between devices  88.6 us (35%)
  other arithmetic  24.4 us (10%)
  local copies, waits for them, and re-layouts  16.1 us (6%)
  between operations  14.8 us (6%)
    all_gather x1, waiting for transfers between devices, local(): collected = lax.all_gather(equations[None], 'gz', axis=0, tiled=True)  69.8 us
    ppermute x10, starting transfers between devices, padded_2(): after = lax.ppermute(leading, axis, down)  35.1 us
    ppermute x10, starting transfers between devices, padded_2(): before = lax.ppermute(last, axis, up)  30.7 us
    ppermute x10, waiting for transfers between devices, padded_2(): after = lax.ppermute(leading, axis, down)  17.3 us
    all_to_all x1, waiting for transfers between devices, solve_rows(): return lax.all_to_all(solved, 'gy', split_axis=1, concat_axis=0, tiled=True)  8.48 us
    all_to_all x1, waiting for transfers between devices, local(): lax.all_to_all(state, 'gy', split_axis=0, concat_axis=1, tiled=True)  8.45 us
    all_to_all x1, starting transfers between devices, local(): lax.all_to_all(state, 'gy', split_axis=0, concat_axis=1, tiled=True)  8.02 us
    all_to_all x1, starting transfers between devices, local(): lax.all_to_all(kappa, 'gy', split_axis=0, concat_axis=1, tiled=True)  7.77 us
  transfers between devices with their start and end apart: 25, of which 12 were waited for; matrix products, arithmetic and copies ran while one was open for 5% of the time, Pallas kernels for 0%

commit v1 on v0

--- a/solution.py
+++ b/solution.py
@@ -145,7 +145,9 @@
     sup_red = -sep_high * following[2]
     rhs_red = lines[depth_z - 1] + sep_low * base[inner_count - 1] + sep_high * following[0]
     equations = jnp.stack([sub_red, diag_red, sup_red, rhs_red])
-    collected = lax.all_gather(equations[None], "gz", axis=0, tiled=True)
+    collected = jnp.concatenate(
+        lax.all_to_all(jnp.stack([equations[None]] * lax.axis_size("gz")), "gz", 0, 0), axis=0
+    )
     values = reduce_lines(collected[:, 0], collected[:, 1], collected[:, 2], (collected[:, 3],), 0)[
         0
     ]

time: 256 us -> 235 us (0.918)
  the two profiles are of different devices: /device:TPU:2 before, /device:TPU:32 now
where the time goes in v1:
time: 235 us; the launch traced here: 233 us
  starting transfers between devices  100 us (43%)
  waiting for transfers between devices  92.3 us (39%)
  other arithmetic  23.8 us (10%)
  local copies, waits for them, and re-layouts  15.5 us (7%)
    all_to_all x1, waiting for transfers between devices, local(): lax.all_to_all(jnp.stack([equations[None]] * lax.axis_size('gz')), 'gz',...  49.5 us
    ppermute x10, starting transfers between devices, padded_2(): before = lax.ppermute(last, axis, up)  37.1 us
    ppermute x10, waiting for transfers between devices, padded_2(): after = lax.ppermute(leading, axis, down)  18.8 us
    ppermute x10, starting transfers between devices, padded_2(): after = lax.ppermute(leading, axis, down)  16.4 us
    all_to_all x1, starting transfers between devices, local(): lax.all_to_all(state, 'gy', split_axis=0, concat_axis=1, tiled=True)  15.4 us
    all_to_all x1, starting transfers between devices, local(): lax.all_to_all(kappa, 'gy', split_axis=0, concat_axis=1, tiled=True)  12.8 us
    all_to_all x1, starting transfers between devices, local(): lax.all_to_all(jnp.stack([equations[None]] * lax.axis_size('gz')), 'gz',...  12.3 us
    all_to_all x1, waiting for transfers between devices, solve_rows(): return lax.all_to_all(solved, 'gy', split_axis=1, concat_axis=0, tiled=True)  9.81 us
  transfers between devices with their start and end apart: 25, of which 11 were waited for; matrix products, arithmetic and copies ran while one was open for 5% of the time, Pallas kernels for 0%

profile of v1, /device:TPU:32, one launch (start us, length us, event | category | flops | bytes accessed | tf_op | source)
XLA Modules:
  0.0 233.3 jit_solution(10036989041179189057)
XLA Ops:
  0.0 0.9 fusion.98
  0.9 3.8 %collective-permute-start.4 = (f32[1,32,128]{2,1,0:T(8,128)S(1)}, f32[1,32,128]{2,1,0:T(8,128)S(1)}, u32[]{:S(2)}, u32[]{:S(2)}) collective-permute-start(f32[1,32,128]{2,1,0:T(8,128)S(1)} %get-tuple-element.204), channel_id=1, source_target_pairs={{0,32},{32,64},{64,96},{96,128},{128,160},{160,192},{192,224},{224... | collective-permute-start | bytes 49160 | tf_op jit(solution)/shard_map/ppermute | solution.py:17
  4.7 0.8 pad_maximum_fusion.14
  5.5 3.8 %collective-permute-start = (f32[3,1,32,128]{3,2,1,0:T(8,128)S(1)}, f32[3,1,32,128]{3,2,1,0:T(8,128)S(1)}, u32[]{:S(2)}, u32[]{:S(2)}) collective-permute-start(f32[3,1,32,128]{3,2,1,0:T(8,128)S(1)} %get-tuple-element.65), channel_id=1, source_target_pairs={{0,32},{32,64},{64,96},{96,128},{128,160},{160,192},{192,224},{224... | collective-permute-start | bytes 147464 | tf_op jit(solution)/shard_map/ppermute | solution.py:17
  9.3 2.3 collective-permute-start.1
  11.6 1.9 collective-permute-start.5
  13.6 4.4 %collective-permute-done.5 = f32[1,32,128]{2,1,0:T(8,128)S(1)} collective-permute-done((f32[1,32,128]{2,1,0:T(8,128)S(1)}, f32[1,32,128]{2,1,0:T(8,128)S(1)}, u32[]{:S(2)}, u32[]{:S(2)}) %collective-permute-start.5) | collective-permute-done | bytes 16416 | tf_op jit(solution)/shard_map/ppermute | solution.py:18
  18.0 1.3 collective-permute-start.6
  19.3 1.3 collective-permute-start.7
  20.7 1.1 pad_maximum_fusion.11
  21.7 4.8 %collective-permute-start.2 = (f32[3,34,1,128]{3,2,1,0:T(1,128)S(1)}, f32[3,34,1,128]{3,2,1,0:T(1,128)S(1)}, u32[]{:S(2)}, u32[]{:S(2)}) collective-permute-start(f32[3,34,1,128]{3,2,1,0:T(1,128)S(1)} %get-tuple-element.61), channel_id=1, source_target_pairs={{0,1},{1,2},{2,3},{3,4},{4,5},{5,6},{6,7},{7,8},{8,9},{9,10},{10,1... | collective-permute-start | bytes 156680 | tf_op jit(solution)/shard_map/ppermute | solution.py:17
  26.6 1.3 collective-permute-start.3
  28.0 2.9 %collective-permute-done.3 = f32[3,34,1,128]{3,2,1,0:T(1,128)S(1)} collective-permute-done((f32[3,34,1,128]{3,2,1,0:T(1,128)S(1)}, f32[3,34,1,128]{3,2,1,0:T(1,128)S(1)}, u32[]{:S(2)}, u32[]{:S(2)}) %collective-permute-start.3) | collective-permute-done | bytes 52256 | tf_op jit(solution)/shard_map/ppermute | solution.py:18
  31.0 1.4 pad_maximum_fusion
  33.4 3.9 %collective-permute-start.8 = (f32[1,32,128]{2,1,0:T(8,128)S(1)}, f32[1,32,128]{2,1,0:T(8,128)S(1)}, u32[]{:S(2)}, u32[]{:S(2)}) collective-permute-start(f32[1,32,128]{2,1,0:T(8,128)S(1)} %get-tuple-element.201), channel_id=1, source_target_pairs={{0,32},{32,64},{64,96},{96,128},{128,160},{160,192},{192,224},{224... | collective-permute-start | bytes 49160 | tf_op jit(solution)/shard_map/ppermute | solution.py:17
  37.3 1.9 collective-permute-start.9
  39.3 12.8 %all-to-all-start.1 = ((f32[32,32,128]{2,1,0:T(8,128)}), f32[32,32,128]{2,1,0:T(8,128)S(1)}, u32[]{:S(2)}, u32[]{:S(2)}) async-start(f32[32,32,128]{2,1,0:T(8,128)} %param.7), calls=%async_computation.1 | async-start | bytes 1048576 | tf_op jit(solution)/shard_map/all_to_all | solution.py:109
  52.1 2.2 collective-permute-start.10
  54.3 1.3 collective-permute-start.11
  55.6 1.3 add_multiply_fusion
  56.9 1.6 collective-permute-done.11
  59.4 5.1 %collective-permute-start.12 = (f32[1,32,128]{2,1,0:T(8,128)S(1)}, f32[1,32,128]{2,1,0:T(8,128)S(1)}, u32[]{:S(2)}, u32[]{:S(2)}) collective-permute-start(f32[1,32,128]{2,1,0:T(8,128)S(1)} %get-tuple-element.199), channel_id=1, source_target_pairs={{0,32},{32,64},{64,96},{96,128},{128,160},{160,192},{192,224},{224... | collective-permute-start | bytes 49160 | tf_op jit(solution)/shard_map/ppermute | solution.py:17
  64.6 1.9 collective-permute-start.13
  66.6 3.6 %collective-permute-done.13 = f32[1,32,128]{2,1,0:T(8,128)S(1)} collective-permute-done((f32[1,32,128]{2,1,0:T(8,128)S(1)}, f32[1,32,128]{2,1,0:T(8,128)S(1)}, u32[]{:S(2)}, u32[]{:S(2)}) %collective-permute-start.13) | collective-permute-done | bytes 16416 | tf_op jit(solution)/shard_map/ppermute | solution.py:18
  70.2 4.0 %collective-permute-start.14 = (f32[34,1,128]{2,1,0:T(1,128)S(1)}, f32[34,1,128]{2,1,0:T(1,128)S(1)}, u32[]{:S(2)}, u32[]{:S(2)}) collective-permute-start(f32[34,1,128]{2,1,0:T(1,128)S(1)} %get-tuple-element.109), channel_id=1, source_target_pairs={{0,1},{1,2},{2,3},{3,4},{4,5},{5,6},{6,7},{7,8},{8,9},{9,10},{10,1... | collective-permute-start | bytes 52232 | tf_op jit(solution)/shard_map/ppermute | solution.py:17
  74.3 1.3 collective-permute-start.15
  75.6 1.1 pad_slice_fusion.2
  76.6 0.7 collective-permute-done.15
  78.3 4.9 %collective-permute-start.16 = (f32[1,32,128]{2,1,0:T(8,128)S(1)}, f32[1,32,128]{2,1,0:T(8,128)S(1)}, u32[]{:S(2)}, u32[]{:S(2)}) collective-permute-start(f32[1,32,128]{2,1,0:T(8,128)S(1)} %get-tuple-element.197), channel_id=1, source_target_pairs={{0,32},{32,64},{64,96},{96,128},{128,160},{160,192},{192,224},{224... | collective-permute-start | bytes 49160 | tf_op jit(solution)/shard_map/ppermute | solution.py:17
  83.1 1.9 collective-permute-start.17
  85.0 0.8 pad_slice_fusion
  85.9 3.9 %collective-permute-done.17 = f32[1,32,128]{2,1,0:T(8,128)S(1)} collective-permute-done((f32[1,32,128]{2,1,0:T(8,128)S(1)}, f32[1,32,128]{2,1,0:T(8,128)S(1)}, u32[]{:S(2)}, u32[]{:S(2)}) %collective-permute-start.17) | collective-permute-done | bytes 16416 | tf_op jit(solution)/shard_map/ppermute | solution.py:18
  89.8 3.2 %collective-permute-start.18 = (f32[34,1,128]{2,1,0:T(1,128)S(1)}, f32[34,1,128]{2,1,0:T(1,128)S(1)}, u32[]{:S(2)}, u32[]{:S(2)}) collective-permute-start(f32[34,1,128]{2,1,0:T(1,128)S(1)} %get-tuple-element.107), channel_id=1, source_target_pairs={{0,1},{1,2},{2,3},{3,4},{4,5},{5,6},{6,7},{7,8},{8,9},{9,10},{10,1... | collective-permute-start | bytes 52232 | tf_op jit(solution)/shard_map/ppermute | solution.py:17
  93.0 1.3 collective-permute-start.19
  94.3 0.7 fusion.44
  95.1 1.7 collective-permute-done.19
  97.4 1.1 fusion.11
  98.5 15.4 %all-to-all-start = ((f32[32,32,128]{2,1,0:T(8,128)}), f32[32,32,128]{2,1,0:T(8,128)S(1)}, u32[]{:S(2)}, u32[]{:S(2)}) async-start(f32[32,32,128]{2,1,0:T(8,128)} %fusion.11), calls=%async_computation | async-start | bytes 1048576 | tf_op jit(solution)/shard_map/all_to_all | solution.py:108
  114.2 1.1 pad_slice_fusion.5
  115.3 9.6 %all-to-all-done = f32[32,32,128]{2,1,0:T(8,128)S(1)} async-done(((f32[32,32,128]{2,1,0:T(8,128)}), f32[32,32,128]{2,1,0:T(8,128)S(1)}, u32[]{:S(2)}, u32[]{:S(2)}) %all-to-all-start) | async-done | bytes 524320 | tf_op jit(solution)/shard_map/all_to_all | solution.py:108
  124.9 0.4 multiply_add_fusion.16
  125.6 0.9 copy-done.7
  126.6 0.5 multiply_add_fusion.15
  127.7 0.5 multiply_add_fusion.13
  129.7 0.5 multiply_add_fusion.9
  130.8 0.5 multiply_add_fusion.7
  134.1 1.0 add_divide_fusion
  135.2 4.4 %all-to-all-start.2 = ((f32[1,1024,128]{2,0,1:T(1,128)}), f32[1,1024,128]{2,0,1:T(1,128)S(1)}, u32[]{:S(2)}, u32[]{:S(2)}) async-start(f32[1,1024,128]{2,0,1:T(1,128)} %bitcast.8), calls=%async_computation.2 | async-start | bytes 1048576 | tf_op jit(solution)/shard_map/all_to_all | solution.py:90
  139.7 0.9 fusion.58
  140.6 9.8 %all-to-all-done.2 = f32[1,1024,128]{2,0,1:T(1,128)S(1)} async-done(((f32[1,1024,128]{2,0,1:T(1,128)}), f32[1,1024,128]{2,0,1:T(1,128)S(1)}, u32[]{:S(2)}, u32[]{:S(2)}) %all-to-all-start.2) | async-done | bytes 524320 | tf_op jit(solution)/shard_map/all_to_all | solution.py:90
  150.5 0.9 copy-done.12
  152.2 0.8 copy-done.9
  153.3 0.7 multiply_add_fusion.31
  155.0 0.9 multiply_add_fusion.29
  156.8 0.8 multiply_add_fusion.27
  157.9 0.7 multiply_add_fusion.22
  158.8 0.5 add_divide_fusion.3
  159.9 1.9 collective-permute-start.20
  161.8 4.5 %collective-permute-done.20 = f32[3,32,128]{2,1,0:T(8,128)S(1)} collective-permute-done((f32[3,32,128]{2,1,0:T(8,128)S(1)}, f32[3,32,128]{2,1,0:T(8,128)S(1)}, u32[]{:S(2)}, u32[]{:S(2)}) %collective-permute-start.20) | collective-permute-done | bytes 49184 | tf_op jit(solution)/shard_map/ppermute | solution.py:26
  166.3 1.1 stack.31
  167.4 12.3 %all-to-all-start.3 = ((f32[16,1,4,32,128]{4,3,2,1,0:T(8,128)}), f32[16,1,4,32,128]{4,3,2,1,0:T(8,128)S(1)}, u32[]{:S(2)}, u32[]{:S(2)}) async-start(f32[16,1,4,32,128]{4,3,2,1,0:T(8,128)} %stack.31), calls=%async_computation.3 | async-start | bytes 2097152 | tf_op jit(solution)/shard_map/all_to_all | solution.py:149
  179.7 49.5 %all-to-all-done.3 = f32[16,1,4,32,128]{4,3,2,1,0:T(8,128)S(1)} async-done(((f32[16,1,4,32,128]{4,3,2,1,0:T(8,128)}), f32[16,1,4,32,128]{4,3,2,1,0:T(8,128)S(1)}, u32[]{:S(2)}, u32[]{:S(2)}) %all-to-all-start.3) | async-done | bytes 1048608 | tf_op jit(solution)/shard_map/all_to_all | solution.py:149
  231.5 0.7 copy-done.6
  232.4 0.8 pad_maximum_fusion.5
  (186 shorter events, 15.8 us)
Async XLA Ops:
  0.0 13.6 %copy-start.4 = (f32[32,32,128]{2,1,0:T(8,128)S(1)}, f32[32,32,128]{2,1,0:T(8,128)}, u32[]{:S(2)}) copy-start(f32[32,32,128]{2,1,0:T(8,128)} %param.4) | copy-start | bytes 1572868
  0.0 20.7 %copy-start.1 = (f32[32,32,128]{2,1,0:T(8,128)S(1)}, f32[32,32,128]{2,1,0:T(8,128)}, u32[]{:S(2)}) copy-start(f32[32,32,128]{2,1,0:T(8,128)} %param.5) | copy-start | bytes 1572868
  0.0 20.7 %copy-start = (f32[32,32,128]{2,1,0:T(8,128)S(1)}, f32[32,32,128]{2,1,0:T(8,128)}, u32[]{:S(2)}) copy-start(f32[32,32,128]{2,1,0:T(8,128)} %param.6) | copy-start | bytes 1572868
  0.9 12.7 %collective-permute-start.4 = (f32[1,32,128]{2,1,0:T(8,128)S(1)}, f32[1,32,128]{2,1,0:T(8,128)S(1)}, u32[]{:S(2)}, u32[]{:S(2)}) collective-permute-start(f32[1,32,128]{2,1,0:T(8,128)S(1)} %get-tuple-element.204), channel_id=1, source_target_pairs={{0,32},{32,64},{64,96},{96,128},{128,160},{160,192},{192,224},{224... | collective-permute-start | bytes 49160 | tf_op jit(solution)/shard_map/ppermute | solution.py:17
  5.5 15.1 %collective-permute-start = (f32[3,1,32,128]{3,2,1,0:T(8,128)S(1)}, f32[3,1,32,128]{3,2,1,0:T(8,128)S(1)}, u32[]{:S(2)}, u32[]{:S(2)}) collective-permute-start(f32[3,1,32,128]{3,2,1,0:T(8,128)S(1)} %get-tuple-element.65), channel_id=1, source_target_pairs={{0,32},{32,64},{64,96},{96,128},{128,160},{160,192},{192,224},{224... | collective-permute-start | bytes 147464 | tf_op jit(solution)/shard_map/ppermute | solution.py:17
  9.3 11.3 %collective-permute-start.1 = (f32[3,1,32,128]{3,2,1,0:T(8,128)S(1)}, f32[3,1,32,128]{3,2,1,0:T(8,128)S(1)}, u32[]{:S(2)}, u32[]{:S(2)}) collective-permute-start(f32[3,1,32,128]{3,2,1,0:T(8,128)S(1)} %get-tuple-element.66), channel_id=1, source_target_pairs={{32,0},{64,32},{96,64},{128,96},{160,128},{192,160},{224,192},{256... | collective-permute-start | bytes 147464 | tf_op jit(solution)/shard_map/ppermute | solution.py:18
  11.6 6.4 %collective-permute-start.5 = (f32[1,32,128]{2,1,0:T(8,128)S(1)}, f32[1,32,128]{2,1,0:T(8,128)S(1)}, u32[]{:S(2)}, u32[]{:S(2)}) collective-permute-start(f32[1,32,128]{2,1,0:T(8,128)S(1)} %get-tuple-element.203), channel_id=1, source_target_pairs={{32,0},{64,32},{96,64},{128,96},{160,128},{192,160},{224,192},{256... | collective-permute-start | bytes 49160 | tf_op jit(solution)/shard_map/ppermute | solution.py:18
  18.0 9.9 %collective-permute-start.6 = (f32[34,1,128]{2,1,0:T(1,128)S(1)}, f32[34,1,128]{2,1,0:T(1,128)S(1)}, u32[]{:S(2)}, u32[]{:S(2)}) collective-permute-start(f32[34,1,128]{2,1,0:T(1,128)S(1)} %get-tuple-element.113), channel_id=1, source_target_pairs={{0,1},{1,2},{2,3},{3,4},{4,5},{5,6},{6,7},{7,8},{8,9},{9,10},{10,1... | collective-permute-start | bytes 52232 | tf_op jit(solution)/shard_map/ppermute | solution.py:17
  19.3 8.6 %collective-permute-start.7 = (f32[34,1,128]{2,1,0:T(1,128)S(1)}, f32[34,1,128]{2,1,0:T(1,128)S(1)}, u32[]{:S(2)}, u32[]{:S(2)}) collective-permute-start(f32[34,1,128]{2,1,0:T(1,128)S(1)} %get-tuple-element.114), channel_id=1, source_target_pairs={{1,0},{2,1},{3,2},{4,3},{5,4},{6,5},{7,6},{8,7},{9,8},{10,9},{11,1... | collective-permute-start | bytes 52232 | tf_op jit(solution)/shard_map/ppermute | solution.py:18
  21.7 6.3 %collective-permute-start.2 = (f32[3,34,1,128]{3,2,1,0:T(1,128)S(1)}, f32[3,34,1,128]{3,2,1,0:T(1,128)S(1)}, u32[]{:S(2)}, u32[]{:S(2)}) collective-permute-start(f32[3,34,1,128]{3,2,1,0:T(1,128)S(1)} %get-tuple-element.61), channel_id=1, source_target_pairs={{0,1},{1,2},{2,3},{3,4},{4,5},{5,6},{6,7},{7,8},{8,9},{9,10},{10,1... | collective-permute-start | bytes 156680 | tf_op jit(solution)/shard_map/ppermute | solution.py:17
  26.6 4.4 %collective-permute-start.3 = (f32[3,34,1,128]{3,2,1,0:T(1,128)S(1)}, f32[3,34,1,128]{3,2,1,0:T(1,128)S(1)}, u32[]{:S(2)}, u32[]{:S(2)}) collective-permute-start(f32[3,34,1,128]{3,2,1,0:T(1,128)S(1)} %get-tuple-element.62), channel_id=1, source_target_pairs={{1,0},{2,1},{3,2},{4,3},{5,4},{6,5},{7,6},{8,7},{9,8},{10,9},{11,1... | collective-permute-start | bytes 156680 | tf_op jit(solution)/shard_map/ppermute | solution.py:18
  33.4 18.7 %collective-permute-start.8 = (f32[1,32,128]{2,1,0:T(8,128)S(1)}, f32[1,32,128]{2,1,0:T(8,128)S(1)}, u32[]{:S(2)}, u32[]{:S(2)}) collective-permute-start(f32[1,32,128]{2,1,0:T(8,128)S(1)} %get-tuple-element.201), channel_id=1, source_target_pairs={{0,32},{32,64},{64,96},{96,128},{128,160},{160,192},{192,224},{224... | collective-permute-start | bytes 49160 | tf_op jit(solution)/shard_map/ppermute | solution.py:17
  37.3 14.7 %collective-permute-start.9 = (f32[1,32,128]{2,1,0:T(8,128)S(1)}, f32[1,32,128]{2,1,0:T(8,128)S(1)}, u32[]{:S(2)}, u32[]{:S(2)}) collective-permute-start(f32[1,32,128]{2,1,0:T(8,128)S(1)} %get-tuple-element.202), channel_id=1, source_target_pairs={{32,0},{64,32},{96,64},{128,96},{160,128},{192,160},{224,192},{256... | collective-permute-start | bytes 49160 | tf_op jit(solution)/shard_map/ppermute | solution.py:18
  39.3 59.3 %all-to-all-start.1 = ((f32[32,32,128]{2,1,0:T(8,128)}), f32[32,32,128]{2,1,0:T(8,128)S(1)}, u32[]{:S(2)}, u32[]{:S(2)}) async-start(f32[32,32,128]{2,1,0:T(8,128)} %param.7), calls=%async_computation.1 | async-start | bytes 1048576 | tf_op jit(solution)/shard_map/all_to_all | solution.py:109
  52.1 4.8 %collective-permute-start.10 = (f32[34,1,128]{2,1,0:T(1,128)S(1)}, f32[34,1,128]{2,1,0:T(1,128)S(1)}, u32[]{:S(2)}, u32[]{:S(2)}) collective-permute-start(f32[34,1,128]{2,1,0:T(1,128)S(1)} %get-tuple-element.111), channel_id=1, source_target_pairs={{0,1},{1,2},{2,3},{3,4},{4,5},{5,6},{6,7},{7,8},{8,9},{9,10},{10,1... | collective-permute-start | bytes 52232 | tf_op jit(solution)/shard_map/ppermute | solution.py:17
  54.3 4.2 %collective-permute-start.11 = (f32[34,1,128]{2,1,0:T(1,128)S(1)}, f32[34,1,128]{2,1,0:T(1,128)S(1)}, u32[]{:S(2)}, u32[]{:S(2)}) collective-permute-start(f32[34,1,128]{2,1,0:T(1,128)S(1)} %get-tuple-element.112), channel_id=1, source_target_pairs={{1,0},{2,1},{3,2},{4,3},{5,4},{6,5},{7,6},{8,7},{9,8},{10,9},{11,1... | collective-permute-start | bytes 52232 | tf_op jit(solution)/shard_map/ppermute | solution.py:18
  56.9 19.7 %copy-start.2 = (f32[31,32,128]{2,1,0:T(8,128)}, f32[31,32,128]{2,1,0:T(8,128)S(1)}, u32[]{:S(2)}) copy-start(f32[31,32,128]{2,1,0:T(8,128)S(1)} %add_multiply_fusion) | copy-start | bytes 1523716
  59.4 7.1 %collective-permute-start.12 = (f32[1,32,128]{2,1,0:T(8,128)S(1)}, f32[1,32,128]{2,1,0:T(8,128)S(1)}, u32[]{:S(2)}, u32[]{:S(2)}) collective-permute-start(f32[1,32,128]{2,1,0:T(8,128)S(1)} %get-tuple-element.199), channel_id=1, source_target_pairs={{0,32},{32,64},{64,96},{96,128},{128,160},{160,192},{192,224},{224... | collective-permute-start | bytes 49160 | tf_op jit(solution)/shard_map/ppermute | solution.py:17
  64.6 5.6 %collective-permute-start.13 = (f32[1,32,128]{2,1,0:T(8,128)S(1)}, f32[1,32,128]{2,1,0:T(8,128)S(1)}, u32[]{:S(2)}, u32[]{:S(2)}) collective-permute-start(f32[1,32,128]{2,1,0:T(8,128)S(1)} %get-tuple-element.200), channel_id=1, source_target_pairs={{32,0},{64,32},{96,64},{128,96},{160,128},{192,160},{224,192},{256... | collective-permute-start | bytes 49160 | tf_op jit(solution)/shard_map/ppermute | solution.py:18
  70.2 6.4 %collective-permute-start.14 = (f32[34,1,128]{2,1,0:T(1,128)S(1)}, f32[34,1,128]{2,1,0:T(1,128)S(1)}, u32[]{:S(2)}, u32[]{:S(2)}) collective-permute-start(f32[34,1,128]{2,1,0:T(1,128)S(1)} %get-tuple-element.109), channel_id=1, source_target_pairs={{0,1},{1,2},{2,3},{3,4},{4,5},{5,6},{6,7},{7,8},{8,9},{9,10},{10,1... | collective-permute-start | bytes 52232 | tf_op jit(solution)/shard_map/ppermute | solution.py:17
  74.3 3.1 %collective-permute-start.15 = (f32[34,1,128]{2,1,0:T(1,128)S(1)}, f32[34,1,128]{2,1,0:T(1,128)S(1)}, u32[]{:S(2)}, u32[]{:S(2)}) collective-permute-start(f32[34,1,128]{2,1,0:T(1,128)S(1)} %get-tuple-element.110), channel_id=1, source_target_pairs={{1,0},{2,1},{3,2},{4,3},{5,4},{6,5},{7,6},{8,7},{9,8},{10,9},{11,1... | collective-permute-start | bytes 52232 | tf_op jit(solution)/shard_map/ppermute | solution.py:18
  78.3 7.6 %collective-permute-start.16 = (f32[1,32,128]{2,1,0:T(8,128)S(1)}, f32[1,32,128]{2,1,0:T(8,128)S(1)}, u32[]{:S(2)}, u32[]{:S(2)}) collective-permute-start(f32[1,32,128]{2,1,0:T(8,128)S(1)} %get-tuple-element.197), channel_id=1, source_target_pairs={{0,32},{32,64},{64,96},{96,128},{128,160},{160,192},{192,224},{224... | collective-permute-start | bytes 49160 | tf_op jit(solution)/shard_map/ppermute | solution.py:17
  83.1 6.6 %collective-permute-start.17 = (f32[1,32,128]{2,1,0:T(8,128)S(1)}, f32[1,32,128]{2,1,0:T(8,128)S(1)}, u32[]{:S(2)}, u32[]{:S(2)}) collective-permute-start(f32[1,32,128]{2,1,0:T(8,128)S(1)} %get-tuple-element.198), channel_id=1, source_target_pairs={{32,0},{64,32},{96,64},{128,96},{160,128},{192,160},{224,192},{256... | collective-permute-start | bytes 49160 | tf_op jit(solution)/shard_map/ppermute | solution.py:18
  89.8 5.3 %collective-permute-start.18 = (f32[34,1,128]{2,1,0:T(1,128)S(1)}, f32[34,1,128]{2,1,0:T(1,128)S(1)}, u32[]{:S(2)}, u32[]{:S(2)}) collective-permute-start(f32[34,1,128]{2,1,0:T(1,128)S(1)} %get-tuple-element.107), channel_id=1, source_target_pairs={{0,1},{1,2},{2,3},{3,4},{4,5},{5,6},{6,7},{7,8},{8,9},{9,10},{10,1... | collective-permute-start | bytes 52232 | tf_op jit(solution)/shard_map/ppermute | solution.py:17
  93.0 3.8 %collective-permute-start.19 = (f32[34,1,128]{2,1,0:T(1,128)S(1)}, f32[34,1,128]{2,1,0:T(1,128)S(1)}, u32[]{:S(2)}, u32[]{:S(2)}) collective-permute-start(f32[34,1,128]{2,1,0:T(1,128)S(1)} %get-tuple-element.108), channel_id=1, source_target_pairs={{1,0},{2,1},{3,2},{4,3},{5,4},{6,5},{7,6},{8,7},{9,8},{10,9},{11,1... | collective-permute-start | bytes 52232 | tf_op jit(solution)/shard_map/ppermute | solution.py:18
  98.5 26.3 %all-to-all-start = ((f32[32,32,128]{2,1,0:T(8,128)}), f32[32,32,128]{2,1,0:T(8,128)S(1)}, u32[]{:S(2)}, u32[]{:S(2)}) async-start(f32[32,32,128]{2,1,0:T(8,128)} %fusion.11), calls=%async_computation | async-start | bytes 1048576 | tf_op jit(solution)/shard_map/all_to_all | solution.py:108
  125.4 1.0 copy-start.7
  125.4 1.2 copy-start.8
  134.1 5.5 %copy-start.3 = (f32[31,32,128]{2,1,0:T(8,128)S(1)}, f32[31,32,128]{2,1,0:T(8,128)}, u32[]{:S(2)}) copy-start(f32[31,32,128]{2,1,0:T(8,128)} %copy-done.2) | copy-start | bytes 1523716
  135.2 15.2 %all-to-all-start.2 = ((f32[1,1024,128]{2,0,1:T(1,128)}), f32[1,1024,128]{2,0,1:T(1,128)S(1)}, u32[]{:S(2)}, u32[]{:S(2)}) async-start(f32[1,1024,128]{2,0,1:T(1,128)} %bitcast.8), calls=%async_computation.2 | async-start | bytes 1048576 | tf_op jit(solution)/shard_map/all_to_all | solution.py:90
  150.4 1.0 copy-start.12
  152.0 1.0 copy-start.9
  152.0 1.2 copy-start.10
  152.0 1.3 copy-start.11
  159.3 6.9 %copy-start.5 = (f32[31,32,128]{2,1,0:T(8,128)}, f32[31,32,128]{2,1,0:T(8,128)S(1)}, u32[]{:S(2)}) copy-start(f32[31,32,128]{2,1,0:T(8,128)S(1)} %get-tuple-element.60) | copy-start | bytes 1523716
  159.9 6.4 %collective-permute-start.20 = (f32[3,32,128]{2,1,0:T(8,128)S(1)}, f32[3,32,128]{2,1,0:T(8,128)S(1)}, u32[]{:S(2)}, u32[]{:S(2)}) collective-permute-start(f32[3,32,128]{2,1,0:T(8,128)S(1)} %pad_maximum_fusion.15), channel_id=1, source_target_pairs={{32,0},{64,32},{96,64},{128,96},{160,128},{192,160},{224,192},{256... | collective-permute-start | bytes 147464 | tf_op jit(solution)/shard_map/ppermute | solution.py:26
  167.4 61.8 %all-to-all-start.3 = ((f32[16,1,4,32,128]{4,3,2,1,0:T(8,128)}), f32[16,1,4,32,128]{4,3,2,1,0:T(8,128)S(1)}, u32[]{:S(2)}, u32[]{:S(2)}) async-start(f32[16,1,4,32,128]{4,3,2,1,0:T(8,128)} %stack.31), calls=%async_computation.3 | async-start | bytes 2097152 | tf_op jit(solution)/shard_map/all_to_all | solution.py:149
  231.2 1.0 copy-start.6
